TPU v7x, 32 devices: a whole 2x2x4 slice. The times are simulated.
32 devices in a mesh: groups: 2 (over y), blk: 4 (over z), tile: 2 (over x), pair: 2 (over core).
Axes of the slice: x: 2, y: 2, z: 4, core: 2. Of those that a mesh axis runs over, the one named last changes fastest.
Arguments:
- left_tokens: bfloat16 [4, 1536, 768], P(('groups', 'pair'), 'blk', 'tile'), parts along dimension 0, may hold values from -32 to 32
- right_tokens: bfloat16 [4, 1536, 768], P(('groups', 'pair'), 'blk', 'tile'), parts along dimension 0, may hold values from -32 to 32
- self_qkv: bfloat16 [3, 768, 512], P(None, None, 'tile'), may hold values from -1 to 1
- self_out: bfloat16 [512, 768], P('tile'), may hold values from -0.25 to 0.25
- cross_qkv: bfloat16 [3, 768, 512], P(None, None, 'tile'), may hold values from -1 to 1
- cross_out: bfloat16 [512, 768], P('tile'), may hold values from -0.25 to 0.25
- reassemble: bfloat16 [768, 256], P('tile'), may hold values from -0.21875 to 0.21875
- conv_weight: bfloat16 [3, 3, 256, 256], replicated, may hold values from -0.125 to 0.125
Outputs:
- joined: bfloat16 [4, 12, 128, 256], P(('groups', 'pair'), 'blk', 'tile'), parts along dimension 0
There are 2 independent parts, one for each index of `groups`. A program takes and returns all parts, laid end to end along the dimension named above; an argument that names none is the same for every part. Nothing has to cross between parts.
All inputs are finite; a program needn't handle non-finite values.
Results may differ from a plain program's by a relative error of at most 0.018.
Values may be sent and summed in bfloat16 or wider, within the bound.
A program may use at most 64 MiB of HBM per device.

v0:
```python
import jax
import jax.numpy as jnp
from jax import lax
from jax.sharding import PartitionSpec as P

HD = 64
CH = 256
GRID_W = 128


def padded_2(cells, sides, width):
    for axis, dim in sides:
        count = lax.axis_size(axis)
        ends = count - 1
        head = lax.slice_in_dim(cells, 0, width, axis=dim)
        tail = lax.slice_in_dim(cells, cells.shape[dim] - width, cells.shape[dim], axis=dim)
        cells = jnp.concatenate(
            [
                lax.ppermute(tail, axis, [(i, (i + 1) % count) for i in range(ends)]),
                cells,
                lax.ppermute(head, axis, [((i + 1) % count, i) for i in range(ends)]),
            ],
            axis=dim,
        )
    return cells


def layer_norm(values):
    widened = values.astype(jnp.float32)
    centred = widened - jnp.mean(widened, axis=-1, keepdims=True)
    variance = jnp.mean(centred * centred, axis=-1, keepdims=True)
    return (centred * lax.rsqrt(variance + 1e-06)).astype(jnp.bfloat16)


def project_rows(normed, weight):
    return jnp.dot(normed, weight, preferred_element_type=jnp.float32).astype(jnp.bfloat16)


def initial_state(queries):
    query_count = queries.shape[0]
    head_count = queries.shape[1] // HD
    return (
        jnp.full((head_count, query_count), -1e30, jnp.float32),
        jnp.zeros((head_count, query_count), jnp.float32),
        jnp.zeros(queries.shape, jnp.float32),
    )


def attend_keys(running, queries, keys_rows, values_rows):
    maxima, totals, accumulated = running
    query_count = queries.shape[0]
    head_count = queries.shape[1] // HD
    key_count = keys_rows.shape[0]
    scores = jnp.einsum(
        "qhd,khd->hqk",
        queries.reshape(query_count, head_count, HD),
        keys_rows.reshape(key_count, head_count, HD),
        preferred_element_type=jnp.float32,
    ) * HD ** (-0.5)
    new_maxima = jnp.maximum(maxima, jnp.max(scores, axis=2))
    correction = jnp.exp(maxima - new_maxima)
    expanded = jnp.exp(scores - new_maxima[:, :, None])
    totals = totals * correction + jnp.sum(expanded, axis=2)
    mixed = jnp.einsum(
        "hqk,khd->qhd",
        expanded.astype(jnp.bfloat16),
        values_rows.reshape(key_count, head_count, HD),
        preferred_element_type=jnp.float32,
    )
    accumulated = (
        accumulated.reshape(query_count, head_count, HD) * correction.T[:, :, None] + mixed
    )
    return (new_maxima, totals, accumulated.reshape(query_count, head_count * HD))


def fold_keys(running, queries, keys_rows, values_rows):
    key_count = keys_rows.shape[0]
    block_rows = max((divisor for divisor in range(1, 1025) if key_count % divisor == 0))
    if block_rows == key_count:
        return attend_keys(running, queries, keys_rows, values_rows)
    stacked_keys = keys_rows.reshape(key_count // block_rows, block_rows, keys_rows.shape[1])
    stacked_values = values_rows.reshape(key_count // block_rows, block_rows, values_rows.shape[1])

    def step_block(current, blocks):
        return (attend_keys(current, queries, blocks[0], blocks[1]), None)

    result, unused = lax.scan(step_block, running, (stacked_keys, stacked_values))
    return result


def finish_state(running):
    maxima, totals, accumulated = running
    query_count = accumulated.shape[0]
    head_count = accumulated.shape[1] // HD
    normalized = accumulated.reshape(query_count, head_count, HD) / totals.T[:, :, None]
    return normalized.reshape(query_count, head_count * HD).astype(jnp.bfloat16)


def body(
    left_tokens, right_tokens, self_qkv, self_out, cross_qkv, cross_out, reassemble, conv_weight
):
    tiles = lax.axis_size("tile")
    tile_index = lax.axis_index("tile")
    token_count, feature_share = (left_tokens.shape[1], left_tokens.shape[2])
    packed = jnp.concatenate(
        [left_tokens[0].reshape(-1), right_tokens[0].reshape(-1), reassemble.reshape(-1)]
    )
    gathered = lax.all_gather(packed, "tile", axis=0)
    block = token_count * feature_share

    def features(offset):
        return jnp.concatenate(
            [
                gathered[i, offset : offset + block].reshape(token_count, feature_share)
                for i in range(tiles)
            ],
            axis=1,
        )

    left_full = features(0)
    right_full = features(block)
    reassemble_full = gathered[:, 2 * block :].reshape(tiles * reassemble.shape[0], CH)
    left_normed = layer_norm(left_full)
    right_normed = layer_norm(right_full)
    self_query = project_rows(left_normed, self_qkv[0])
    projected = jnp.stack(
        [
            project_rows(left_normed, self_qkv[1]),
            project_rows(left_normed, self_qkv[2]),
            project_rows(right_normed, cross_qkv[1]),
            project_rows(right_normed, cross_qkv[2]),
        ]
    )
    pieces = lax.all_gather(projected, "blk", axis=1, tiled=True)
    self_state = fold_keys(initial_state(self_query), self_query, pieces[0], pieces[1])
    self_mixed = finish_state(self_state)
    self_term = jnp.dot(self_mixed, self_out, preferred_element_type=jnp.float32)
    self_sum = lax.psum(self_term.astype(jnp.bfloat16), "tile").astype(jnp.float32)
    updated = (left_full.astype(jnp.float32) + self_sum).astype(jnp.bfloat16)
    updated_normed = layer_norm(updated)
    cross_query = project_rows(updated_normed, cross_qkv[0])
    cross_state = fold_keys(initial_state(cross_query), cross_query, pieces[2], pieces[3])
    cross_mixed = finish_state(cross_state)
    cross_term = jnp.dot(cross_mixed, cross_out, preferred_element_type=jnp.float32)
    cross_sum = lax.psum(cross_term.astype(jnp.bfloat16), "tile").astype(jnp.float32)
    final_tokens = (updated.astype(jnp.float32) + cross_sum).astype(jnp.bfloat16)
    band_rows = token_count // GRID_W
    column_count = GRID_W // tiles
    grid = jnp.pad(final_tokens.reshape(band_rows, GRID_W, -1), ((0, 0), (1, 1), (0, 0)))
    window = lax.dynamic_slice_in_dim(grid, tile_index * column_count, column_count + 2, axis=1)
    wide_map = (
        jnp.dot(
            window.reshape(band_rows * (column_count + 2), -1),
            reassemble_full,
            preferred_element_type=jnp.float32,
        )
        .astype(jnp.bfloat16)
        .reshape(band_rows, column_count + 2, CH)
    )
    feature_map = wide_map[:, 1 : column_count + 1]
    activated = jnp.maximum(wide_map, jnp.zeros((), jnp.bfloat16))
    padded = padded_2(activated, (("blk", 0),), 1)
    stacked = jnp.concatenate(
        [
            padded[row_shift : row_shift + band_rows, col_shift : col_shift + column_count]
            for row_shift in range(3)
            for col_shift in range(3)
        ],
        axis=-1,
    )
    convolved = jnp.dot(
        stacked.reshape(band_rows * column_count, 9 * CH),
        conv_weight.reshape(9 * CH, CH),
        preferred_element_type=jnp.float32,
    )
    joined = (
        feature_map.astype(jnp.float32) + convolved.reshape(band_rows, column_count, CH)
    ).astype(jnp.bfloat16)
    return joined[None]


def solution(mesh):
    placed = (
        P(("groups", "pair"), "blk", "tile"),
        P(("groups", "pair"), "blk", "tile"),
        P(None, None, "tile"),
        P("tile", None),
        P(None, None, "tile"),
        P("tile", None),
        P("tile", None),
        P(),
    )
    return jax.shard_map(
        body,
        mesh=mesh,
        in_specs=placed,
        out_specs=P(("groups", "pair"), "blk", "tile", None),
        check_vma=False,
    )
```

profile of v0, /device:TPU:0, one launch (start us, length us, event | category | flops | bytes accessed | tf_op | source)
XLA Modules:
  0.0 234.0 jit_solution(1149109852763883605)
XLA Ops:
  10.0 30.0 %all-gather.6.cloned.1.call-done = bf16[786432]{0:T(1024)(128)(2,1)} async-done(((bf16[393216]{0:T(1024)(128)(2,1)}), bf16[786432]{0:T(1024)(128)(2,1)}) %all-gather.6.cloned.1.call-update) | async-done | bytes 1572880 | tf_op jit(solution)/shard_map/all_gather | solution.py:108
  40.0 1.8 reshape.110
  41.9 7.2 %slice_reduce_fusion.3 = (bf16[147456]{0:T(1024)(128)(2,1)S(1)}, bf16[147456]{0:T(1024)(128)(2,1)}, bf16[147456]{0:T(1024)(128)(2,1)}, bf16[147456]{0:T(1024)(128)(2,1)S(1)}) fusion(bf16[2,393216]{1,0:T(2,128)(2,1)S(1)} %reshape.110), kind=kLoop, calls=%fused_computation.80 | loop fusion | bytes 2359296 | tf_op jit(solution)/shard_map/slice | solution.py:114
  51.7 1.4 fusion.49
  53.1 1.4 fusion.48
  57.9 1.3 convolution_convert_fusion.3
  59.4 62.0 %all-gather.4.cloned.1.call-done = bf16[4,1536,256]{2,1,0:T(8,128)(2,1)} async-done(((bf16[4,384,256]{2,1,0:T(8,128)(2,1)}), bf16[4,1536,256]{2,1,0:T(8,128)(2,1)}) %all-gather.4.cloned.1.call-update) | async-done | bytes 3145744 | tf_op jit(solution)/shard_map/all_gather | solution.py:134
  121.5 3.3 %fusion.82 = (bf16[1,1536,256]{2,1,0:T(8,128)(2,1)S(1)}, bf16[1,1536,256]{2,1,0:T(8,128)(2,1)}, bf16[1,1536,256]{2,1,0:T(8,128)(2,1)}, bf16[1,1536,256]{2,1,0:T(8,128)(2,1)}) fusion(bf16[4,1536,256]{2,1,0:T(8,128)(2,1)} %all-gather.4.cloned.1.call-done), kind=kLoop, calls=%fused_computation.131 | loop fusion | bytes 6291456 | tf_op jit(solution)/shard_map/slice | solution.py:142
  124.8 11.9 %while.30 = (s32[]{:T(128)}, f32[4,384]{1,0:T(4,128)S(1)}, f32[4,384]{1,0:T(4,128)S(1)}, f32[384,256]{0,1:T(8,128)S(1)}, bf16[2,768,256]{2,1,0:T(8,128)(2,1)}, /...) while((s32[]{:T(128)}, f32[4,384]{1,0:T(4,128)S(1)}, ...), condition=%wide.region_7.8_spmd.clone, body=%wide.region_4.7_spmd.clone.sunk | while | flops 311632896 | bytes 20742316 | solution.py:87
  127.0 1.8 bitcast_reduce_fusion.4
  132.9 1.8 bitcast_reduce_fusion.4
  136.7 2.2 convolution_convert_fusion.1
  139.2 28.6 %all-reduce.4.cloned.1.call-done = bf16[384,768]{1,0:T(8,128)(2,1)} async-done(((bf16[384,768]{1,0:T(8,128)(2,1)}), bf16[384,768]{1,0:T(8,128)(2,1)}) %all-reduce.4.cloned.1.call-update) | async-done | bytes 589840 | tf_op jit(solution)/shard_map/psum | solution.py:138
  167.8 1.3 convert_reduce_fusion
  169.5 1.4 convolution_convert_fusion.2
  171.1 11.6 %while.31 = (s32[]{:T(128)}, f32[4,384]{1,0:T(4,128)S(1)}, f32[4,384]{1,0:T(4,128)S(1)}, f32[384,256]{0,1:T(8,128)S(1)}, bf16[2,768,256]{2,1,0:T(8,128)(2,1)}, /...) while((s32[]{:T(128)}, f32[4,384]{1,0:T(4,128)S(1)}, ...), condition=%wide.region_14.15_spmd.clone, body=%wide.region_11.14_spmd.clone.sunk | while | flops 311632896 | bytes 20742316 | solution.py:87
  173.2 1.8 bitcast_reduce_fusion.5
  179.0 1.8 bitcast_reduce_fusion.5
  182.8 2.3 convolution_convert_fusion
  185.3 30.0 %all-reduce.6.cloned.1.call-done = bf16[384,768]{1,0:T(8,128)(2,1)} async-done(((bf16[384,768]{1,0:T(8,128)(2,1)}), bf16[384,768]{1,0:T(8,128)(2,1)}) %all-reduce.6.cloned.1.call-update) | async-done | bytes 589840 | tf_op jit(solution)/shard_map/psum | solution.py:145
  215.3 1.2 fusion.45
  217.0 3.4 %collective-permute-start = (bf16[1,66,256]{2,1,0:T(8,128)(2,1)S(1)}, bf16[1,66,256]{2,1,0:T(8,128)(2,1)S(1)}, u32[]{:S(2)}, u32[]{:S(2)}) collective-permute-start(bf16[1,66,256]{2,1,0:T(8,128)(2,1)S(1)} %get-tuple-element.212), channel_id=1, source_target_pairs={{0,4},{4,8},{8,12},{1,5},{5,9},{9,13},{2,6},{6,10},{10,14},{3,7},{... | collective-permute-start | bytes 101384 | tf_op jit(solution)/shard_map/ppermute | solution.py:19
  220.4 1.3 collective-permute-start.1
  222.2 4.1 %collective-permute-done.1 = bf16[1,66,256]{2,1,0:T(8,128)(2,1)S(1)} collective-permute-done((bf16[1,66,256]{2,1,0:T(8,128)(2,1)S(1)}, bf16[1,66,256]{2,1,0:T(8,128)(2,1)S(1)}, u32[]{:S(2)}, u32[]{:S(2)}) %collective-permute-start.1) | collective-permute-done | bytes 33824 | tf_op jit(solution)/shard_map/ppermute | solution.py:21
  (129 shorter events, 29.0 us)
Async XLA Ops:
  6.5 219.8 %copy-start = (bf16[3,3,256,256]{3,2,1,0:T(8,128)(2,1)S(1)}, bf16[3,3,256,256]{3,2,1,0:T(8,128)(2,1)}, u32[]{:S(2)}) copy-start(bf16[3,3,256,256]{3,2,1,0:T(8,128)(2,1)} %param.19) | copy-start | bytes 3538948
  6.5 2.3 copy-start.12
  6.5 33.5 %all-gather.6.cloned.1.call-start = ((), (), s32[]{:S(2)}) async-start(), calls=%async_computation.3 | async-start | bytes 2359296 | tf_op jit(solution)/shard_map/all_gather | solution.py:108
  10.0 111.5 %all-gather.4.cloned.1.call-start = ((), (), s32[]{:S(2)}) async-start(), calls=%async_computation | async-start | bytes 3932160 | tf_op jit(solution)/shard_map/all_gather | solution.py:134
  41.8 7.2 %copy-start.1 = (bf16[2,393216]{1,0:T(2,128)(2,1)}, bf16[2,393216]{1,0:T(2,128)(2,1)S(1)}, u32[]{:S(2)}) copy-start(bf16[2,393216]{1,0:T(2,128)(2,1)S(1)} %reshape.110) | copy-start | bytes 4718596
  54.7 0.9 copy-start.2
  54.8 0.8 copy-start.4
  54.8 1.4 copy-start.13
  57.9 110.0 %all-reduce.4.cloned.1.call-start = ((), (), s32[]{:S(2)}) async-start(), calls=%async_computation.1 | async-start | bytes 1179648 | tf_op jit(solution)/shard_map/psum | solution.py:138
  124.8 0.7 copy-start.6
  129.8 0.9 copy-start.7
  135.7 0.9 copy-start.7
  136.7 31.2 %copy-start.3 = (bf16[384,384]{1,0:T(8,128)(2,1)S(1)}, bf16[384,384]{1,0:T(8,128)(2,1)}, u32[]{:S(2)}) copy-start(bf16[384,384]{1,0:T(8,128)(2,1)} %copy-done.2) | copy-start | bytes 884740
  136.7 31.2 %copy-start.5 = (bf16[384,384]{1,0:T(8,128)(2,1)S(1)}, bf16[384,384]{1,0:T(8,128)(2,1)}, u32[]{:S(2)}) copy-start(bf16[384,384]{1,0:T(8,128)(2,1)} %copy-done.4) | copy-start | bytes 884740
  139.0 76.3 %all-reduce.6.cloned.1.call-start = ((), (), s32[]{:S(2)}) async-start(), calls=%async_computation.2 | async-start | bytes 1179648 | tf_op jit(solution)/shard_map/psum | solution.py:145
  169.2 1.7 copy-start.10
  171.1 0.7 copy-start.8
  176.0 0.9 copy-start.9
  176.9 0.7 copy-start.8
  181.8 0.9 copy-start.9
  182.8 2.3 slice-start
  185.0 30.3 %copy-start.11 = (bf16[384,768]{1,0:T(8,128)(2,1)S(1)}, bf16[384,768]{1,0:T(8,128)(2,1)}, u32[]{:S(2)}) copy-start(bf16[384,768]{1,0:T(8,128)(2,1)} %copy-done.10) | copy-start | bytes 1769476
  217.0 5.0 %collective-permute-start = (bf16[1,66,256]{2,1,0:T(8,128)(2,1)S(1)}, bf16[1,66,256]{2,1,0:T(8,128)(2,1)S(1)}, u32[]{:S(2)}, u32[]{:S(2)}) collective-permute-start(bf16[1,66,256]{2,1,0:T(8,128)(2,1)S(1)} %get-tuple-element.212), channel_id=1, source_target_pairs={{0,4},{4,8},{8,12},{1,5},{5,9},{9,13},{2,6},{6,10},{10,14},{3,7},{... | collective-permute-start | bytes 101384 | tf_op jit(solution)/shard_map/ppermute | solution.py:19
  220.4 5.9 %collective-permute-start.1 = (bf16[1,66,256]{2,1,0:T(8,128)(2,1)S(1)}, bf16[1,66,256]{2,1,0:T(8,128)(2,1)S(1)}, u32[]{:S(2)}, u32[]{:S(2)}) collective-permute-start(bf16[1,66,256]{2,1,0:T(8,128)(2,1)S(1)} %get-tuple-element.211), channel_id=1, source_target_pairs={{4,0},{8,4},{12,8},{5,1},{9,5},{13,9},{6,2},{10,6},{14,10},{7,3},{... | collective-permute-start | bytes 101384 | tf_op jit(solution)/shard_map/ppermute | solution.py:21
  (1 other events, 0.7 us)
Sparse Core Ops, SparseCore 0:
  10.1 29.8 all-gather.5
  58.0 63.4 all-gather.3
  139.1 28.7 all-reduce.3
  185.2 30.0 all-reduce.5
where the time goes:
time: 235 us; the launch traced here: 234 us
  waiting for transfers between devices  155 us (66%)
  local copies, waits for them, and re-layouts  27.7 us (12%)
  matrix products  23 us (10%)
  between operations  13.5 us (6%)
  other arithmetic  9.46 us (4%)
  starting transfers between devices  4.99 us (2%)
    all_gather x1, waiting for transfers between devices, body(): pieces = lax.all_gather(projected, 'blk', axis=1, tiled=True)  62 us
    all_gather x1, waiting for transfers between devices, body(): gathered = lax.all_gather(packed, 'tile', axis=0)  30 us
    psum x1, waiting for transfers between devices, body(): lax.psum(cross_term.astype(jnp.bfloat16), 'tile').astype(jnp.float32)  30 us
    psum x1, waiting for transfers between devices, body(): lax.psum(self_term.astype(jnp.bfloat16), 'tile').astype(jnp.float32)  28.6 us
    slice x1, local copies, waits for them, and re-layouts, features(): gathered[i, offset:offset + block].reshape(token_count, feature_share)  7.18 us
    dot_general x4, matrix products, attend_keys(): jnp.einsum('qhd,khd->hqk', queries.reshape(query_count, head_count, HD),...  7.05 us
    dot_general x6, matrix products, project_rows(): jnp.dot(normed, weight, preferred_element_type=jnp.float32)  6.08 us
    dynamic_slice x12, local copies, waits for them, and re-layouts, fold_keys(): lax.scan(step_block, running, (stacked_keys, stacked_values))  5.79 us
  transfers between devices with their start and end apart: 6, of which 6 were waited for; matrix products, arithmetic and copies ran while one was open for 1% of the time, Pallas kernels for 0%

commit v1 on v0

--- a/solution.py
+++ b/solution.py
@@ -6,6 +6,23 @@
 HD = 64
 CH = 256
 GRID_W = 128
+
+
+def joined_along(parts, dim):
+    lengths = list(parts.shape[1:])
+    lengths[dim] *= parts.shape[0]
+    return jnp.moveaxis(parts, 0, dim).reshape(lengths)
+
+
+def doubled(x, axis):
+    size, index = (lax.axis_size(axis), lax.axis_index(axis))
+    tiles, distance = (x[None], 1)
+    while distance < size:
+        other = lax.ppermute(tiles, axis, [(i, i ^ distance) for i in range(size)])
+        low = index & distance == 0
+        tiles = jnp.concatenate([jnp.where(low, tiles, other), jnp.where(low, other, tiles)])
+        distance *= 2
+    return tiles
 
 
 def padded_2(cells, sides, width):
@@ -131,7 +148,7 @@
             project_rows(right_normed, cross_qkv[2]),
         ]
     )
-    pieces = lax.all_gather(projected, "blk", axis=1, tiled=True)
+    pieces = joined_along(doubled(projected, "blk"), 1)
     self_state = fold_keys(initial_state(self_query), self_query, pieces[0], pieces[1])
     self_mixed = finish_state(self_state)
     self_term = jnp.dot(self_mixed, self_out, preferred_element_type=jnp.float32)

time: 235 us -> 264 us (1.12)
  waiting for transfers between devices: 155 us -> 178 us
  starting transfers between devices: 4.99 us -> 8.86 us
  other arithmetic: 9.46 us -> 13.2 us
    ppermute x0 -> x2, waiting for transfers between devices: none -> 83.9 us  [doubled(): other = lax.ppermute(tiles, axis, [(i, i ^ distance) for i in range(size)])]
    all_gather x1 -> x0, waiting for transfers between devices: 62 us -> none  [body(): pieces = lax.all_gather(projected, 'blk', axis=1, tiled=True)]
    ppermute x0 -> x2, starting transfers between devices: none -> 3.91 us  [doubled(): other = lax.ppermute(tiles, axis, [(i, i ^ distance) for i in range(size)])]
    select_n x0 -> x2, other arithmetic: none -> 3.09 us  [doubled(): jnp.where(low, tiles, other)]
  transfers between devices with their start and end apart: 6 -> 7, of which waited for: 6 -> 7; matrix products, arithmetic and copies ran while one was open for 1% -> 1% of each run, Pallas kernels for 0% -> 0%
where the time goes in v1:
time: 264 us; the launch traced here: 263 us
  waiting for transfers between devices  178 us (67%)
  local copies, waits for them, and re-layouts  26.1 us (10%)
  matrix products  22.9 us (9%)
  between operations  13.5 us (5%)
  other arithmetic  13.2 us (5%)
  starting transfers between devices  8.86 us (3%)
    ppermute x2, waiting for transfers between devices, doubled(): other = lax.ppermute(tiles, axis, [(i, i ^ distance) for i in range(size)])  83.9 us
    all_gather x1, waiting for transfers between devices, body(): gathered = lax.all_gather(packed, 'tile', axis=0)  30 us
    psum x1, waiting for transfers between devices, body(): lax.psum(self_term.astype(jnp.bfloat16), 'tile').astype(jnp.float32)  30 us
    psum x1, waiting for transfers between devices, body(): lax.psum(cross_term.astype(jnp.bfloat16), 'tile').astype(jnp.float32)  30 us
    slice x1, local copies, waits for them, and re-layouts, features(): gathered[i, offset:offset + block].reshape(token_count, feature_share)  7.19 us
    dot_general x4, matrix products, attend_keys(): jnp.einsum('qhd,khd->hqk', queries.reshape(query_count, head_count, HD),...  7.05 us
    dot_general x6, matrix products, project_rows(): jnp.dot(normed, weight, preferred_element_type=jnp.float32)  6.07 us
    dynamic_slice x12, local copies, waits for them, and re-layouts, fold_keys(): lax.scan(step_block, running, (stacked_keys, stacked_values))  5.79 us
  transfers between devices with their start and end apart: 7, of which 7 were waited for; matrix products, arithmetic and copies ran while one was open for 1% of the time, Pallas kernels for 0%

profile of v1, /device:TPU:0, one launch (start us, length us, event | category | flops | bytes accessed | tf_op | source)
XLA Modules:
  0.0 263.2 jit_solution(10436239818872464787)
XLA Ops:
  10.0 30.0 %all-gather.3.cloned.1.call-done = bf16[786432]{0:T(1024)(128)(2,1)} async-done(((bf16[393216]{0:T(1024)(128)(2,1)}), bf16[786432]{0:T(1024)(128)(2,1)}) %all-gather.3.cloned.1.call-update) | async-done | bytes 1572880 | tf_op jit(solution)/shard_map/all_gather | solution.py:125
  40.0 1.8 reshape.119
  41.9 7.2 %slice_reduce_fusion.3 = (bf16[147456]{0:T(1024)(128)(2,1)S(1)}, bf16[147456]{0:T(1024)(128)(2,1)}, bf16[147456]{0:T(1024)(128)(2,1)}, bf16[147456]{0:T(1024)(128)(2,1)S(1)}) fusion(bf16[2,393216]{1,0:T(2,128)(2,1)S(1)} %reshape.119), kind=kLoop, calls=%fused_computation.86 | loop fusion | bytes 2359296 | tf_op jit(solution)/shard_map/slice | solution.py:131
  51.8 1.4 fusion.49
  57.2 1.5 collective-permute-start
  58.7 17.7 %collective-permute-done = bf16[1,4,384,256]{3,2,1,0:T(8,128)(2,1)} collective-permute-done((bf16[1,4,384,256]{3,2,1,0:T(8,128)(2,1)S(1)}, bf16[1,4,384,256]{3,2,1,0:T(8,128)(2,1)}, u32[]{:S(2)}, u32[]{:S(2)}) %collective-permute-start) | collective-permute-done | bytes 786464 | tf_op jit(solution)/shard_map/ppermute | solution.py:21
  76.5 1.5 broadcast_select_fusion.3
  79.2 2.4 collective-permute-start.1
  83.1 66.1 %collective-permute-done.1 = bf16[2,4,384,256]{3,2,1,0:T(8,128)(2,1)} collective-permute-done((bf16[2,4,384,256]{3,2,1,0:T(8,128)(2,1)}, bf16[2,4,384,256]{3,2,1,0:T(8,128)(2,1)}, u32[]{:S(2)}, u32[]{:S(2)}) %collective-permute-start.1) | collective-permute-done | bytes 1572896 | tf_op jit(solution)/shard_map/ppermute | solution.py:21
  149.3 1.6 broadcast_select_fusion.1
  151.2 1.4 fusion.82
  152.6 11.9 %while.30 = (s32[]{:T(128)}, f32[4,384]{1,0:T(4,128)S(1)}, f32[4,384]{1,0:T(4,128)S(1)}, f32[384,256]{0,1:T(8,128)S(1)}, bf16[2,768,256]{2,1,0:T(8,128)(2,1)}, /...) while((s32[]{:T(128)}, f32[4,384]{1,0:T(4,128)S(1)}, ...), condition=%wide.region_7.8_spmd.clone, body=%wide.region_4.7_spmd.clone.sunk | while | flops 311632896 | bytes 20742316 | solution.py:104
  154.9 1.8 bitcast_reduce_fusion.4
  160.8 1.8 bitcast_reduce_fusion.4
  164.6 2.2 convolution_convert_fusion.1
  167.1 30.0 %all-reduce.4.cloned.1.call-done = bf16[384,768]{1,0:T(8,128)(2,1)} async-done(((bf16[384,768]{1,0:T(8,128)(2,1)}), bf16[384,768]{1,0:T(8,128)(2,1)}) %all-reduce.4.cloned.1.call-update) | async-done | bytes 589840 | tf_op jit(solution)/shard_map/psum | solution.py:155
  198.7 1.4 convolution_convert_fusion.2
  200.3 11.7 %while.31 = (s32[]{:T(128)}, f32[4,384]{1,0:T(4,128)S(1)}, f32[4,384]{1,0:T(4,128)S(1)}, f32[384,256]{0,1:T(8,128)S(1)}, bf16[2,768,256]{2,1,0:T(8,128)(2,1)}, /...) while((s32[]{:T(128)}, f32[4,384]{1,0:T(4,128)S(1)}, ...), condition=%wide.region_14.15_spmd.clone, body=%wide.region_11.14_spmd.clone.sunk | while | flops 311632896 | bytes 20742316 | solution.py:104
  202.4 1.8 bitcast_reduce_fusion.5
  208.3 1.8 bitcast_reduce_fusion.5
  212.1 2.2 convolution_convert_fusion
  214.6 30.0 %all-reduce.6.cloned.1.call-done = bf16[384,768]{1,0:T(8,128)(2,1)} async-done(((bf16[384,768]{1,0:T(8,128)(2,1)}), bf16[384,768]{1,0:T(8,128)(2,1)}) %all-reduce.6.cloned.1.call-update) | async-done | bytes 589840 | tf_op jit(solution)/shard_map/psum | solution.py:162
  246.3 3.4 %collective-permute-start.2 = (bf16[1,66,256]{2,1,0:T(8,128)(2,1)S(1)}, bf16[1,66,256]{2,1,0:T(8,128)(2,1)S(1)}, u32[]{:S(2)}, u32[]{:S(2)}) collective-permute-start(bf16[1,66,256]{2,1,0:T(8,128)(2,1)S(1)} %get-tuple-element.216), channel_id=1, source_target_pairs={{0,4},{4,8},{8,12},{1,5},{5,9},{9,13},{2,6},{6,10},{10,14},{3,7},{... | collective-permute-start | bytes 101384 | tf_op jit(solution)/shard_map/ppermute | solution.py:36
  251.5 4.1 %collective-permute-done.3 = bf16[1,66,256]{2,1,0:T(8,128)(2,1)S(1)} collective-permute-done((bf16[1,66,256]{2,1,0:T(8,128)(2,1)S(1)}, bf16[1,66,256]{2,1,0:T(8,128)(2,1)S(1)}, u32[]{:S(2)}, u32[]{:S(2)}) %collective-permute-start.3) | collective-permute-done | bytes 33824 | tf_op jit(solution)/shard_map/ppermute | solution.py:38
  (144 shorter events, 36.4 us)
Async XLA Ops:
  6.5 249.1 %copy-start = (bf16[3,3,256,256]{3,2,1,0:T(8,128)(2,1)S(1)}, bf16[3,3,256,256]{3,2,1,0:T(8,128)(2,1)}, u32[]{:S(2)}) copy-start(bf16[3,3,256,256]{3,2,1,0:T(8,128)(2,1)} %param.19) | copy-start | bytes 3538948
  6.5 2.3 copy-start.17
  6.5 33.5 %all-gather.3.cloned.1.call-start = ((), (), s32[]{:S(2)}) async-start(), calls=%async_computation.2 | async-start | bytes 2359296 | tf_op jit(solution)/shard_map/all_gather | solution.py:125
  10.0 187.1 %all-reduce.4.cloned.1.call-start = ((), (), s32[]{:S(2)}) async-start(), calls=%async_computation | async-start | bytes 1179648 | tf_op jit(solution)/shard_map/psum | solution.py:155
  41.9 7.2 %copy-start.1 = (bf16[2,393216]{1,0:T(2,128)(2,1)}, bf16[2,393216]{1,0:T(2,128)(2,1)S(1)}, u32[]{:S(2)}) copy-start(bf16[2,393216]{1,0:T(2,128)(2,1)S(1)} %reshape.119) | copy-start | bytes 4718596
  54.5 2.4 copy-start.12
  54.7 0.9 copy-start.2
  54.8 1.4 copy-start.18
  57.1 1.7 copy-start.14
  57.2 19.2 %collective-permute-start = (bf16[1,4,384,256]{3,2,1,0:T(8,128)(2,1)S(1)}, bf16[1,4,384,256]{3,2,1,0:T(8,128)(2,1)}, u32[]{:S(2)}, u32[]{:S(2)}) collective-permute-start(bf16[1,4,384,256]{3,2,1,0:T(8,128)(2,1)S(1)} %maximum_bitcast_fusion.1), channel_id=1, source_target_pairs={{0,4},{4,0},{8,12},{12,8},{1,5},{5,1},{9,13},{13,9},{2,6},{6,2},{1... | collective-permute-start | bytes 2359304 | tf_op jit(solution)/shard_map/ppermute | solution.py:21
  77.9 3.7 %copy-start.16 = (bf16[384,768]{1,0:T(8,128)(2,1)S(1)}, bf16[384,768]{1,0:T(8,128)(2,1)}, u32[]{:S(2)}) copy-start(bf16[384,768]{1,0:T(8,128)(2,1)} %copy-done.15) | copy-start | bytes 1769476
  79.2 70.0 %collective-permute-start.1 = (bf16[2,4,384,256]{3,2,1,0:T(8,128)(2,1)}, bf16[2,4,384,256]{3,2,1,0:T(8,128)(2,1)}, u32[]{:S(2)}, u32[]{:S(2)}) collective-permute-start(bf16[2,4,384,256]{3,2,1,0:T(8,128)(2,1)} %pad_maximum_fusion), channel_id=1, source_target_pairs={{0,8},{4,12},{8,0},{12,4},{1,9},{5,13},{9,1},{13,5},{2,10},{6,14},... | collective-permute-start | bytes 4718600 | tf_op jit(solution)/shard_map/ppermute | solution.py:21
  157.7 0.9 copy-start.7
  163.6 0.9 copy-start.7
  164.5 32.5 %copy-start.3 = (bf16[384,384]{1,0:T(8,128)(2,1)S(1)}, bf16[384,384]{1,0:T(8,128)(2,1)}, u32[]{:S(2)}) copy-start(bf16[384,384]{1,0:T(8,128)(2,1)} %copy-done.2) | copy-start | bytes 884740
  164.5 32.5 %copy-start.5 = (bf16[384,384]{1,0:T(8,128)(2,1)S(1)}, bf16[384,384]{1,0:T(8,128)(2,1)}, u32[]{:S(2)}) copy-start(bf16[384,384]{1,0:T(8,128)(2,1)} %copy-done.4) | copy-start | bytes 884740
  166.8 77.7 %all-reduce.6.cloned.1.call-start = ((), (), s32[]{:S(2)}) async-start(), calls=%async_computation.1 | async-start | bytes 1179648 | tf_op jit(solution)/shard_map/psum | solution.py:162
  198.4 1.7 copy-start.10
  205.2 0.9 copy-start.9
  211.1 0.9 copy-start.9
  212.0 2.3 slice-start
  214.3 30.3 %copy-start.11 = (bf16[384,768]{1,0:T(8,128)(2,1)S(1)}, bf16[384,768]{1,0:T(8,128)(2,1)}, u32[]{:S(2)}) copy-start(bf16[384,768]{1,0:T(8,128)(2,1)} %copy-done.10) | copy-start | bytes 1769476
  246.3 5.0 %collective-permute-start.2 = (bf16[1,66,256]{2,1,0:T(8,128)(2,1)S(1)}, bf16[1,66,256]{2,1,0:T(8,128)(2,1)S(1)}, u32[]{:S(2)}, u32[]{:S(2)}) collective-permute-start(bf16[1,66,256]{2,1,0:T(8,128)(2,1)S(1)} %get-tuple-element.216), channel_id=1, source_target_pairs={{0,4},{4,8},{8,12},{1,5},{5,9},{9,13},{2,6},{6,10},{10,14},{3,7},{... | collective-permute-start | bytes 101384 | tf_op jit(solution)/shard_map/ppermute | solution.py:36
  249.7 5.9 %collective-permute-start.3 = (bf16[1,66,256]{2,1,0:T(8,128)(2,1)S(1)}, bf16[1,66,256]{2,1,0:T(8,128)(2,1)S(1)}, u32[]{:S(2)}, u32[]{:S(2)}) collective-permute-start(bf16[1,66,256]{2,1,0:T(8,128)(2,1)S(1)} %get-tuple-element.215), channel_id=1, source_target_pairs={{4,0},{8,4},{12,8},{5,1},{9,5},{13,9},{6,2},{10,6},{14,10},{7,3},{... | collective-permute-start | bytes 101384 | tf_op jit(solution)/shard_map/ppermute | solution.py:38
  (7 other events, 5.0 us)
Sparse Core Ops, SparseCore 0:
  10.1 29.8 all-gather.2
  167.0 30.0 all-reduce.3
  214.4 30.0 all-reduce.5
